TPU v7x, 128 devices: a whole 4x4x4 slice. The times are simulated.
128 devices in a mesh: dp: 64 (over y_hi, z, x, core), col: 2 (over y_lo).
Axes of the slice: x: 4, y: 4 (y_hi: 2, y_lo: 2; y = y_hi * 2 + y_lo), z: 4, core: 2. Of those that a mesh axis runs over, the one named last changes fastest.
Arguments:
- tokens: bfloat16 [8192, 2048], P('dp'), may hold values from -6 to 6
- routes: int32 [8192, 8], P('dp'), may hold values from 0 to 127, all different within a row; in each aligned block of 128 rows (0 to 127, 128 to 255, ...) at most 12 rows name the same one
- probs: float32 [8192, 8], P('dp'), may hold values from 0.1 to 1
- w_gate: bfloat16 [128, 2048, 768], P('dp', None, 'col'), may hold values from -0.125 to 0.125
- w_up: bfloat16 [128, 2048, 768], P('dp', None, 'col'), may hold values from -0.125 to 0.125
- w_down: bfloat16 [128, 768, 2048], P('dp', 'col'), may hold values from -0.21875 to 0.21875
- cotangent: bfloat16 [8192, 2048], P('dp', 'col'), may hold values from -6 to 6
Outputs:
- mixed: bfloat16 [8192, 2048], P('dp', 'col')
- grad_tokens: bfloat16 [8192, 2048], P('dp', 'col')
- grad_probs: float32 [8192, 8], P('dp')
- grad_gate: bfloat16 [128, 2048, 768], P('dp', None, 'col')
- grad_up: bfloat16 [128, 2048, 768], P('dp', None, 'col')
- grad_down: bfloat16 [128, 768, 2048], P('dp', 'col')
Inputs may be any that keep to these rules, and one draw needn't show every extreme that they name: `routes`: each token names 8 different experts. Among the 128 tokens of one index of dp, no expert is named by more than 12 of them, a bound that some block reaches.
All inputs are finite; a program needn't handle non-finite values.
Results may differ from a plain program's by a relative error of at most 0.0064.
Values may be sent and summed in bfloat16 or wider, within the bound.
A program may use at most 192 MiB of HBM per device.

v0:
```python
import jax
import jax.numpy as jnp
from jax import lax
from jax.sharding import PartitionSpec as P


def body(tokens, routes, probs, w_gate, w_up, w_down, cotangent):
    tok_count, width = tokens.shape
    top_count = routes.shape[1]
    owners = lax.axis_size("dp")
    local_experts = w_gate.shape[0]
    experts = local_experts * owners
    slot_cap = 3 * tok_count * top_count // (2 * experts)
    half_width = width // lax.axis_size("col")
    flat_routes = routes.reshape(-1)
    expert_ids = jnp.arange(experts, dtype=jnp.int32)
    onehot = (flat_routes[:, None] == expert_ids[None, :]).astype(jnp.int32)
    before = jnp.cumsum(onehot, axis=0) - onehot
    slot_index = jnp.sum(before * onehot, axis=1)
    flat_index = flat_routes * slot_cap + slot_index

    def scatter_rows(row_pairs):
        buffer = jnp.zeros((experts * slot_cap, row_pairs.shape[1]), row_pairs.dtype)
        buffer = buffer.at[flat_index].set(row_pairs)
        return buffer.reshape(owners, local_experts * slot_cap, row_pairs.shape[1])

    def send_whole(row_pairs):
        return lax.all_to_all(
            scatter_rows(row_pairs), "dp", split_axis=0, concat_axis=0, tiled=True
        )

    def send_back(partial_value):
        summed = lax.psum_scatter(partial_value, "col", scatter_dimension=2, tiled=True).astype(
            jnp.bfloat16
        )
        returned = lax.all_to_all(summed, "dp", split_axis=0, concat_axis=0, tiled=True)
        return returned.reshape(experts * slot_cap, half_width)[flat_index].reshape(
            tok_count, top_count, half_width
        )

    arrived_rows = send_whole(jnp.repeat(tokens, top_count, axis=0))
    row_block = arrived_rows.reshape(owners, local_experts, slot_cap, width)
    gate_acts = jnp.einsum("slcd,ldh->slch", row_block, w_gate, preferred_element_type=jnp.float32)
    up_acts = jnp.einsum("slcd,ldh->slch", row_block, w_up, preferred_element_type=jnp.float32)
    sigmoid_g = jax.nn.sigmoid(gate_acts)
    silu_g = gate_acts * sigmoid_g
    hidden = (silu_g * up_acts).astype(jnp.bfloat16)
    out_partial = jnp.einsum("slch,lhd->slcd", hidden, w_down, preferred_element_type=jnp.float32)
    picked_out = send_back(out_partial.reshape(owners, local_experts * slot_cap, width))
    picked_wide = picked_out.astype(jnp.float32)
    mixed = jnp.sum(probs[:, :, None] * picked_wide, axis=1).astype(jnp.bfloat16)
    cot_wide = cotangent.astype(jnp.float32)
    prob_part = jnp.sum(cot_wide[:, None, :] * picked_wide, axis=2)
    full_cot = lax.all_gather(cotangent, "col", axis=1, tiled=True)
    scaled_full = (probs[:, :, None] * full_cot.astype(jnp.float32)[:, None, :]).astype(
        jnp.bfloat16
    )
    arrived_cot = send_whole(scaled_full.reshape(tok_count * top_count, width))
    d_out = arrived_cot.reshape(owners, local_experts, slot_cap, width)
    grad_down = jnp.einsum(
        "slch,slcd->lhd", hidden, d_out, preferred_element_type=jnp.float32
    ).astype(jnp.bfloat16)
    d_hidden = jnp.einsum("slcd,lhd->slch", d_out, w_down, preferred_element_type=jnp.float32)
    d_gate = (d_hidden * up_acts * sigmoid_g * (1.0 + gate_acts * (1.0 - sigmoid_g))).astype(
        jnp.bfloat16
    )
    d_up = (d_hidden * silu_g).astype(jnp.bfloat16)
    grad_gate = jnp.einsum(
        "slcd,slch->ldh", row_block, d_gate, preferred_element_type=jnp.float32
    ).astype(jnp.bfloat16)
    grad_up = jnp.einsum(
        "slcd,slch->ldh", row_block, d_up, preferred_element_type=jnp.float32
    ).astype(jnp.bfloat16)
    d_partial = jnp.einsum(
        "slch,ldh->slcd", d_gate, w_gate, preferred_element_type=jnp.float32
    ) + jnp.einsum("slch,ldh->slcd", d_up, w_up, preferred_element_type=jnp.float32)
    picked_grad = send_back(d_partial.reshape(owners, local_experts * slot_cap, width))
    grad_tokens = jnp.sum(picked_grad.astype(jnp.float32), axis=1).astype(jnp.bfloat16)
    grad_probs = lax.psum(prob_part, "col")
    return (mixed, grad_tokens, grad_probs, grad_gate, grad_up, grad_down)


def solution(mesh):
    return jax.shard_map(
        body,
        mesh=mesh,
        in_specs=(
            P("dp", None),
            P("dp", None),
            P("dp", None),
            P("dp", None, "col"),
            P("dp", None, "col"),
            P("dp", "col", None),
            P("dp", "col"),
        ),
        out_specs=(
            P("dp", "col"),
            P("dp", "col"),
            P("dp", None),
            P("dp", None, "col"),
            P("dp", None, "col"),
            P("dp", "col", None),
        ),
        check_vma=False,
    )
```

profile of v0, /device:TPU:10, one launch (start us, length us, event | category | flops | bytes accessed | tf_op | source)
XLA Modules:
  0.0 687.5 jit_solution(13827045977689101927)
XLA Ops:
  7.2 0.8 broadcast_multiply_fusion
  8.0 0.9 copy.29
  8.9 0.1 eq.29
  9.1 0.1 copy.28
  9.2 0.1 mul.81
  9.3 0.1 copy.31
  9.4 0.2 fusion.34
  9.6 0.8 copy-done.8
  10.4 1.1 broadcast_add_fusion
  11.5 0.1 copy.32
  11.6 0.4 fusion.33
  12.0 10.6 %scatter_custom_fusion = bf16[1536,2048]{1,0:T(8,128)(2,1)} fusion(s32[1024]{0:T(1024)S(1)} %bitcast.136, bf16[]{:T(256)} %constant.6.clone.1, bf16[128,2048]{1,0:T(8,128)(2,1)} %param.7), kind=kCustom, calls=%fused_computation.15 | custom fusion | bytes 6815746 | tf_op jit(solution)/shard_map/scatter | solution.py:24
  22.6 10.9 %all-to-all-start = ((bf16[64,24,2048]{2,1,0:T(8,128)(2,1)}), bf16[64,24,2048]{2,1,0:T(8,128)(2,1)}, u32[]{:S(2)}, u32[]{:S(2)}) async-start(bf16[64,24,2048]{2,1,0:T(8,128)(2,1)} %bitcast.126), calls=%async_computation | async-start | bytes 12582912 | tf_op jit(solution)/shard_map/all_to_all | solution.py:28
  33.5 0.1 copy.27
  33.6 0.1 mul.86
  33.7 87.4 %all_gather.3 = bf16[128,2048]{1,0:T(8,128)(2,1)S(1)} all-gather(bf16[128,1024]{1,0:T(8,128)(2,1)S(1)} %copy-done.11), channel_id=1, replica_groups=mesh['dp'=64,'col'=2] {'col'}, dimensions={1}, use_global_device_ids=true | all-gather | bytes 786432 | tf_op jit(solution)/shard_map/all_gather | solution.py:54
  121.1 1.1 convert_element_type.63
  122.2 11.0 %scatter_custom_fusion.1 = bf16[1536,2048]{1,0:T(8,128)(2,1)} fusion(s32[1024]{0:T(1024)S(1)} %bitcast.137, f32[128,2048]{1,0:T(8,128)} %convert_element_type.63, f32[1024]{0:T(1024)S(1)} %mul.86, bf16[]{:T(256)} %constant.6.clone.1), kind=kCustom, calls=%fused_computation.14 | custom fusion | flops 4194304 | bytes 7344130 | tf_op jit(solution)/shard_map/scatter | solution.py:24
  133.2 10.4 %all-to-all-start.2 = ((bf16[64,24,2048]{2,1,0:T(8,128)(2,1)}), bf16[64,24,2048]{2,1,0:T(8,128)(2,1)}, u32[]{:S(2)}, u32[]{:S(2)}) async-start(bf16[64,24,2048]{2,1,0:T(8,128)(2,1)} %bitcast.125), calls=%async_computation.3 | async-start | bytes 12582912 | tf_op jit(solution)/shard_map/all_to_all | solution.py:28
  143.6 0.2 reduce-scatter.5.cloned.1.call-start
  143.9 6.4 copy.33
  150.3 4.8 fusion.10
  155.1 4.8 fusion.14
  159.9 66.7 %all-to-all-done.2 = bf16[64,24,2048]{2,1,0:T(8,128)(2,1)} async-done(((bf16[64,24,2048]{2,1,0:T(8,128)(2,1)}), bf16[64,24,2048]{2,1,0:T(8,128)(2,1)}, u32[]{:S(2)}, u32[]{:S(2)}) %all-to-all-start.2) | async-done | bytes 6291488 | tf_op jit(solution)/shard_map/all_to_all | solution.py:28
  226.7 6.4 copy.36
  233.1 6.0 fusion.25
  239.1 4.9 fusion.12
  244.0 7.7 %convolution_add_fusion = f32[2,64,12,2048]{3,1,2,0:T(8,128)} fusion(f32[2,64,12,2048]{3,1,2,0:T(8,128)S(1)} %fusion.12, bf16[64,2,12,384]{3,0,2,1:T(8,128)(2,1)} %get-tuple-element.14, bf16[2,2048,384]{2,1,0:T(8,128)(2,1)S(1)} %copy-done.7), kind=kOutput, calls=%fused_computation.9 | convolution fusion | flops 2419064832 | bytes 29491200 | tf_op jit(solution)/shard_map/slch,ldh->slcd/dot_general | solution.py:76
  251.8 16.4 %copy.37 = f32[64,24,2048]{2,1,0:T(8,128)} copy(f32[64,24,2048]{2,0,1:T(8,128)} %bitcast.124) | data formatting | bytes 25165824 | tf_op jit(solution)/shard_map/reshape | solution.py:77
  268.2 7.9 %fusion.18 = f32[2,64,12,2048]{3,1,2,0:T(8,128)} fusion(bf16[64,2,12,384]{3,0,2,1:T(8,128)(2,1)} %get-tuple-element.16, bf16[2,384,2048]{2,1,0:T(8,128)(2,1)S(1)} %copy-done), kind=kOutput, calls=%fused_computation.28 | convolution fusion | flops 2415919104 | bytes 16908288 | tf_op jit(solution)/shard_map/slch,lhd->slcd/dot_general | solution.py:48
  276.2 17.3 %copy.34 = f32[64,24,2048]{2,1,0:T(8,128)} copy(f32[64,24,2048]{2,0,1:T(8,128)} %bitcast.123) | data formatting | bytes 25165824 | tf_op jit(solution)/shard_map/reshape | solution.py:49
  293.5 123.5 %reduce-scatter.5.cloned.1.call-done = f32[64,24,1024]{2,1,0:T(8,128)} async-done(((f32[64,24,2048]{2,1,0:T(8,128)}), f32[64,24,1024]{2,1,0:T(8,128)}) %reduce-scatter.5.cloned.1.call-update) | async-done | bytes 6291472 | tf_op jit(solution)/shard_map/reduce_scatter | solution.py:33
  417.1 4.9 convert_element_type.67
  422.0 9.8 %all-to-all-start.3 = ((bf16[64,24,1024]{2,1,0:T(8,128)(2,1)}), bf16[64,24,1024]{2,1,0:T(8,128)(2,1)S(1)}, u32[]{:S(2)}, u32[]{:S(2)}) async-start(bf16[64,24,1024]{2,1,0:T(8,128)(2,1)} %convert_element_type.67), calls=%async_computation.5 | async-start | bytes 6291456 | tf_op jit(solution)/shard_map/all_to_all | solution.py:36
  431.8 0.8 convert_element_type.68
  432.7 170.9 %reduce-scatter.3.cloned.1.call-done = f32[64,24,1024]{2,1,0:T(8,128)} async-done(((f32[64,24,2048]{2,1,0:T(8,128)}), f32[64,24,1024]{2,1,0:T(8,128)}) %reduce-scatter.3.cloned.1.call-update) | async-done | bytes 6291472 | tf_op jit(solution)/shard_map/reduce_scatter | solution.py:33
  603.6 4.9 convert_element_type.59
  608.5 7.9 %all-to-all-start.1 = ((bf16[64,24,1024]{2,1,0:T(8,128)(2,1)}), bf16[64,24,1024]{2,1,0:T(8,128)(2,1)}, u32[]{:S(2)}, u32[]{:S(2)}) async-start(bf16[64,24,1024]{2,1,0:T(8,128)(2,1)} %convert_element_type.59), calls=%async_computation.2 | async-start | bytes 6291456 | tf_op jit(solution)/shard_map/all_to_all | solution.py:36
  616.5 7.6 %bitcast_convert_fusion = bf16[2,384,2048]{2,1,0:T(8,128)(2,1)} fusion(bf16[64,2,12,384]{3,0,2,1:T(8,128)(2,1)} %get-tuple-element.16, bf16[64,2,12,2048]{3,0,2,1:T(8,128)(2,1)} %bitcast.134), kind=kOutput, calls=%fused_computation.6 | convolution fusion | flops 2417491968 | bytes 10616832 | tf_op jit(solution)/shard_map/slch,slcd->lhd/dot_general | solution.py:60
  624.1 8.1 %bitcast_convert_fusion.1 = bf16[2,2048,384]{2,1,0:T(8,128)(2,1)} fusion(bf16[64,2,12,2048]{3,0,2,1:T(8,128)(2,1)} %bitcast.129, bf16[64,2,12,384]{3,0,2,1:T(8,128)(2,1)S(1)} %copy-done.10), kind=kOutput, calls=%fused_computation.7 | convolution fusion | flops 2417491968 | bytes 10616832 | tf_op jit(solution)/shard_map/slcd,slch->ldh/dot_general | solution.py:71
  632.2 4.9 bitcast_convert_fusion.2
  637.1 5.4 gather_fusion.1
  642.5 3.7 bitcast_reduce_fusion
  646.2 11.5 %all-to-all-done.1 = bf16[64,24,1024]{2,1,0:T(8,128)(2,1)} async-done(((bf16[64,24,1024]{2,1,0:T(8,128)(2,1)}), bf16[64,24,1024]{2,1,0:T(8,128)(2,1)}, u32[]{:S(2)}, u32[]{:S(2)}) %all-to-all-start.1) | async-done | bytes 3145760 | tf_op jit(solution)/shard_map/all_to_all | solution.py:36
  657.7 8.5 %gather_fusion = bf16[1024,1024]{1,0:T(8,128)(2,1)} fusion(bf16[1536,1024]{1,0:T(8,128)(2,1)} %bitcast.18, s32[1024]{0:T(1024)S(1)} %broadcast_clamp_fusion), kind=kCustom, calls=%fused_computation | custom fusion | bytes 4198400 | tf_op jit(solution)/shard_map/gather | solution.py:37
  666.2 4.1 fusion.2
  670.2 9.6 %psum.7 = f32[128,8]{1,0:T(8,128)S(1)} all-reduce(f32[128,8]{1,0:T(8,128)S(1)} %get-tuple-element.12), channel_id=1, replica_groups=mesh['dp'=64,'col'=2] {'col'}, use_global_device_ids=true, to_apply=%region_10.11 | all-reduce | flops 1024 | bytes 8192 | tf_op jit(solution)/shard_map/psum | solution.py:79
  679.8 0.7 copy.38
  (45 shorter events, 0.3 us)
Async XLA Ops:
  7.2 225.9 %copy-start = (bf16[2,384,2048]{2,1,0:T(8,128)(2,1)S(1)}, bf16[2,384,2048]{2,1,0:T(8,128)(2,1)}, u32[]{:S(2)}) copy-start(bf16[2,384,2048]{2,1,0:T(8,128)(2,1)} %param.12) | copy-start | bytes 9437188
  9.6 0.8 copy-start.8
  22.6 10.9 %copy-start.12 = (f32[128,8]{0,1:T(8,128)S(1)}, f32[128,8]{0,1:T(8,128)}, u32[]{:S(2)}) copy-start(f32[128,8]{0,1:T(8,128)} %param.9) | copy-start | bytes 12292
  22.6 11.1 %copy-start.11 = (bf16[128,1024]{1,0:T(8,128)(2,1)S(1)}, bf16[128,1024]{1,0:T(8,128)(2,1)}, u32[]{:S(2)}) copy-start(bf16[128,1024]{1,0:T(8,128)(2,1)} %param.13) | copy-start | bytes 786436
  22.6 110.6 %all-to-all-start = ((bf16[64,24,2048]{2,1,0:T(8,128)(2,1)}), bf16[64,24,2048]{2,1,0:T(8,128)(2,1)}, u32[]{:S(2)}, u32[]{:S(2)}) async-start(bf16[64,24,2048]{2,1,0:T(8,128)(2,1)} %bitcast.126), calls=%async_computation | async-start | bytes 12582912 | tf_op jit(solution)/shard_map/all_to_all | solution.py:28
  133.2 93.5 %all-to-all-start.2 = ((bf16[64,24,2048]{2,1,0:T(8,128)(2,1)}), bf16[64,24,2048]{2,1,0:T(8,128)(2,1)}, u32[]{:S(2)}, u32[]{:S(2)}) async-start(bf16[64,24,2048]{2,1,0:T(8,128)(2,1)} %bitcast.125), calls=%async_computation.3 | async-start | bytes 12582912 | tf_op jit(solution)/shard_map/all_to_all | solution.py:28
  143.6 273.4 %reduce-scatter.5.cloned.1.call-start = ((), (), s32[]{:S(2)}) async-start(), calls=%async_computation.7 | async-start | bytes 18874368 | tf_op jit(solution)/shard_map/reduce_scatter | solution.py:33
  143.9 6.4 copy-start.6
  150.3 4.8 copy-start.2
  150.3 4.8 copy-start.4
  226.7 6.4 copy-start.13
  226.7 6.4 copy-start.14
  233.1 6.1 copy-start.3
  233.1 6.0 copy-start.5
  239.1 4.9 copy-start.7
  268.2 335.4 %reduce-scatter.3.cloned.1.call-start = ((), (), s32[]{:S(2)}) async-start(), calls=%async_computation.6 | async-start | bytes 18874368 | tf_op jit(solution)/shard_map/reduce_scatter | solution.py:33
  422.0 186.5 %all-to-all-start.3 = ((bf16[64,24,1024]{2,1,0:T(8,128)(2,1)}), bf16[64,24,1024]{2,1,0:T(8,128)(2,1)S(1)}, u32[]{:S(2)}, u32[]{:S(2)}) async-start(bf16[64,24,1024]{2,1,0:T(8,128)(2,1)} %convert_element_type.67), calls=%async_computation.5 | async-start | bytes 6291456 | tf_op jit(solution)/shard_map/all_to_all | solution.py:36
  608.5 49.1 %all-to-all-start.1 = ((bf16[64,24,1024]{2,1,0:T(8,128)(2,1)}), bf16[64,24,1024]{2,1,0:T(8,128)(2,1)}, u32[]{:S(2)}, u32[]{:S(2)}) async-start(bf16[64,24,1024]{2,1,0:T(8,128)(2,1)} %convert_element_type.59), calls=%async_computation.2 | async-start | bytes 6291456 | tf_op jit(solution)/shard_map/all_to_all | solution.py:36
  616.5 7.6 %copy-start.10 = (bf16[64,2,12,384]{3,0,2,1:T(8,128)(2,1)S(1)}, bf16[64,2,12,384]{3,0,2,1:T(8,128)(2,1)}, u32[]{:S(2)}) copy-start(bf16[64,2,12,384]{3,0,2,1:T(8,128)(2,1)} %get-tuple-element.14) | copy-start | bytes 3538948
  616.5 15.7 %slice-start = ((s8[6291456]{0:T(1024)(128)(4,1)}), s8[4194304]{0:T(1024)(128)(4,1)S(1)}, s32[]{:S(2)}) async-start(s8[6291456]{0:T(1024)(128)(4,1)} %bitcast.130), calls=%async_computation.8 | async-start | bytes 8388608
  624.1 8.1 %slice-start.1 = ((s8[6291456]{0:T(1024)(128)(4,1)}), s8[2097152]{0:T(1024)(128)(4,1)S(1)}, s32[]{:S(2)}) async-start(s8[6291456]{0:T(1024)(128)(4,1)} %bitcast.130), calls=%async_computation.9 | async-start | bytes 4194304
  624.1 8.1 %copy-start.9 = (bf16[64,2,12,384]{3,0,2,1:T(8,128)(2,1)S(1)}, bf16[64,2,12,384]{3,0,2,1:T(8,128)(2,1)}, u32[]{:S(2)}) copy-start(bf16[64,2,12,384]{3,0,2,1:T(8,128)(2,1)} %get-tuple-element.15) | copy-start | bytes 3538948
  657.7 22.8 %copy-start.1 = (bf16[2,384,2048]{2,1,0:T(8,128)(2,1)S(1)}, bf16[2,384,2048]{2,1,0:T(8,128)(2,1)}, u32[]{:S(2)}) copy-start(bf16[2,384,2048]{2,1,0:T(8,128)(2,1)} %param.12) | copy-start | bytes 9437188
Sparse Core Ops, SparseCore 0:
  268.3 148.7 reduce-scatter.4
  419.5 184.0 reduce-scatter.2
where the time goes:
time: 694 us; the launch traced here: 688 us
  waiting for transfers between devices  373 us (54%)
  blocking collectives  96.9 us (14%)
  local copies, waits for them, and re-layouts  74.1 us (11%)
  matrix products  56.8 us (8%)
  starting transfers between devices  39.3 us (6%)
  other arithmetic  33.1 us (5%)
  between operations  14.5 us (2%)
    reduce_scatter x2, waiting for transfers between devices, send_back(): lax.psum_scatter(partial_value, 'col', scatter_dimension=2, tiled=True)  294 us
    all_gather x1, blocking collectives, body(): full_cot = lax.all_gather(cotangent, 'col', axis=1, tiled=True)  87.4 us
    all_to_all x2, waiting for transfers between devices, send_whole(): lax.all_to_all(scatter_rows(row_pairs), 'dp', split_axis=0, concat_axis=0...  66.7 us
    all_to_all x2, starting transfers between devices, send_whole(): lax.all_to_all(scatter_rows(row_pairs), 'dp', split_axis=0, concat_axis=0...  21.3 us
    all_to_all x2, starting transfers between devices, send_back(): lax.all_to_all(summed, 'dp', split_axis=0, concat_axis=0, tiled=True)  17.7 us
    reshape x1, local copies, waits for them, and re-layouts, body(): out_partial.reshape(owners, local_experts * slot_cap, width)  17.3 us
    reshape x1, local copies, waits for them, and re-layouts, body(): d_partial.reshape(owners, local_experts * slot_cap, width)  16.4 us
  transfers between devices with their start and end apart: 6, of which 4 were waited for; matrix products, arithmetic and copies ran while one was open for 14% of the time, Pallas kernels for 0%

commit v1 on v0

--- a/solution.py
+++ b/solution.py
@@ -1,7 +1,19 @@
+import functools
 import jax
 import jax.numpy as jnp
 from jax import lax
 from jax.sharding import PartitionSpec as P
+
+
+def draw_sizes_over_axis(u_in, dim_at):
+    arr_next = lax.all_to_all(
+        jnp.stack(tuple((u_in for _ in range(lax.axis_size("col"))))), "col", 0, 0
+    )
+    work_now = jnp.concatenate(arr_next, axis=dim_at)
+    return work_now
+
+
+rest_the_space = functools.partial(draw_sizes_over_axis, dim_at=1)
 
 
 def body(tokens, routes, probs, w_gate, w_up, w_down, cotangent):
@@ -51,7 +63,7 @@
     mixed = jnp.sum(probs[:, :, None] * picked_wide, axis=1).astype(jnp.bfloat16)
     cot_wide = cotangent.astype(jnp.float32)
     prob_part = jnp.sum(cot_wide[:, None, :] * picked_wide, axis=2)
-    full_cot = lax.all_gather(cotangent, "col", axis=1, tiled=True)
+    full_cot = rest_the_space(cotangent)
     scaled_full = (probs[:, :, None] * full_cot.astype(jnp.float32)[:, None, :]).astype(
         jnp.bfloat16
     )

time: 694 us -> 685 us (0.987)
  blocking collectives: 96.9 us -> 9.55 us
  waiting for transfers between devices: 373 us -> 442 us
    all_gather x1 -> x0, blocking collectives: 87.4 us -> none  [body(): full_cot = lax.all_gather(cotangent, 'col', axis=1, tiled=True)]
    all_to_all x2, waiting for transfers between devices: 66.7 us -> 134 us  [send_whole(): lax.all_to_all(scatter_rows(row_pairs), 'dp', split_axis=0, concat_axis=0...]
  transfers between devices with their start and end apart: 6 -> 7, of which waited for: 4 -> 5; matrix products, arithmetic and copies ran while one was open for 14% -> 16% of each run, Pallas kernels for 0% -> 0%
where the time goes in v1:
time: 685 us; the launch traced here: 678 us
  waiting for transfers between devices  442 us (65%)
  local copies, waits for them, and re-layouts  76.8 us (11%)
  matrix products  57 us (8%)
  starting transfers between devices  43.4 us (6%)
  other arithmetic  34.8 us (5%)
  between operations  14.5 us (2%)
  blocking collectives  9.55 us (1%)
    reduce_scatter x2, waiting for transfers between devices, send_back(): lax.psum_scatter(partial_value, 'col', scatter_dimension=2, tiled=True)  297 us
    all_to_all x2, waiting for transfers between devices, send_whole(): lax.all_to_all(scatter_rows(row_pairs), 'dp', split_axis=0, concat_axis=0...  134 us
    all_to_all x2, starting transfers between devices, send_whole(): lax.all_to_all(scatter_rows(row_pairs), 'dp', split_axis=0, concat_axis=0...  20.6 us
    all_to_all x2, starting transfers between devices, send_back(): lax.all_to_all(summed, 'dp', split_axis=0, concat_axis=0, tiled=True)  17.9 us
    reshape x1, local copies, waits for them, and re-layouts, body(): d_partial.reshape(owners, local_experts * slot_cap, width)  16.4 us
    reshape x1, local copies, waits for them, and re-layouts, body(): out_partial.reshape(owners, local_experts * slot_cap, width)  16.3 us
    gather x2, local copies, waits for them, and re-layouts, send_back(): returned.reshape(experts * slot_cap, half_width)[flat_index]  13.8 us
  transfers between devices with their start and end apart: 7, of which 5 were waited for; matrix products, arithmetic and copies ran while one was open for 16% of the time, Pallas kernels for 0%

profile of v1, /device:TPU:10, one launch (start us, length us, event | category | flops | bytes accessed | tf_op | source)
XLA Modules:
  0.0 678.1 jit_solution(123122084829586388)
XLA Ops:
  7.2 1.3 copy.38
  8.5 0.8 pad_maximum_fusion
  9.3 4.6 all-to-all-start.2
  13.9 0.7 broadcast_multiply_fusion
  14.6 0.8 copy.31
  15.6 0.1 copy.33
  15.7 0.2 fusion.34
  15.9 0.8 copy-done.8
  16.7 1.1 broadcast_add_fusion
  17.8 0.1 copy.34
  17.9 0.4 fusion.33
  18.3 0.1 copy.30
  18.5 10.6 %scatter_custom_fusion = bf16[1536,2048]{1,0:T(8,128)(2,1)} fusion(s32[1024]{0:T(1024)S(1)} %bitcast.142, bf16[]{:T(256)} %constant.6.clone.1, bf16[128,2048]{1,0:T(8,128)(2,1)} %param.7), kind=kCustom, calls=%fused_computation.15 | custom fusion | bytes 6815746 | tf_op jit(solution)/shard_map/scatter | solution.py:36
  29.1 11.8 %all-to-all-start = ((bf16[64,24,2048]{2,1,0:T(8,128)(2,1)}), bf16[64,24,2048]{2,1,0:T(8,128)(2,1)}, u32[]{:S(2)}, u32[]{:S(2)}) async-start(bf16[64,24,2048]{2,1,0:T(8,128)(2,1)} %bitcast.129), calls=%async_computation | async-start | bytes 12582912 | tf_op jit(solution)/shard_map/all_to_all | solution.py:40
  41.2 2.1 convert_element_type.86
  43.2 2.5 copy.39
  45.8 11.0 %scatter_custom_fusion.1 = bf16[1536,2048]{1,0:T(8,128)(2,1)} fusion(s32[1024]{0:T(1024)S(1)} %bitcast.143, f32[128,2048]{1,0:T(8,128)} %copy.39, f32[1024]{0:T(1024)S(1)} %mul.86, bf16[]{:T(256)} %constant.6.clone.1), kind=kCustom, calls=%fused_computation.14 | custom fusion | flops 4194304 | bytes 7344130 | tf_op jit(solution)/shard_map/scatter | solution.py:36
  56.8 66.8 %all-to-all-done = bf16[64,24,2048]{2,1,0:T(8,128)(2,1)} async-done(((bf16[64,24,2048]{2,1,0:T(8,128)(2,1)}), bf16[64,24,2048]{2,1,0:T(8,128)(2,1)}, u32[]{:S(2)}, u32[]{:S(2)}) %all-to-all-start) | async-done | bytes 6291488 | tf_op jit(solution)/shard_map/all_to_all | solution.py:40
  123.6 8.8 %all-to-all-start.3 = ((bf16[64,24,2048]{2,1,0:T(8,128)(2,1)}), bf16[64,24,2048]{2,1,0:T(8,128)(2,1)}, u32[]{:S(2)}, u32[]{:S(2)}) async-start(bf16[64,24,2048]{2,1,0:T(8,128)(2,1)} %bitcast.130), calls=%async_computation.4 | async-start | bytes 12582912 | tf_op jit(solution)/shard_map/all_to_all | solution.py:40
  132.4 0.2 reduce-scatter.5.cloned.1.call-start
  132.7 6.4 copy.35
  139.1 4.8 fusion.10
  143.9 4.8 fusion.14
  148.7 66.7 %all-to-all-done.3 = bf16[64,24,2048]{2,1,0:T(8,128)(2,1)} async-done(((bf16[64,24,2048]{2,1,0:T(8,128)(2,1)}), bf16[64,24,2048]{2,1,0:T(8,128)(2,1)}, u32[]{:S(2)}, u32[]{:S(2)}) %all-to-all-start.3) | async-done | bytes 6291488 | tf_op jit(solution)/shard_map/all_to_all | solution.py:40
  215.5 6.4 copy.40
  221.9 6.0 fusion.25
  227.9 4.9 fusion.12
  232.8 7.8 %convolution_add_fusion = f32[2,64,12,2048]{3,1,2,0:T(8,128)} fusion(f32[2,64,12,2048]{3,1,2,0:T(8,128)S(1)} %fusion.12, bf16[64,2,12,384]{3,0,2,1:T(8,128)(2,1)} %get-tuple-element.14, bf16[2,2048,384]{2,1,0:T(8,128)(2,1)S(1)} %copy-done.7), kind=kOutput, calls=%fused_computation.9 | convolution fusion | flops 2419064832 | bytes 29491200 | tf_op jit(solution)/shard_map/slch,ldh->slcd/dot_general | solution.py:88
  240.6 16.4 %copy.41 = f32[64,24,2048]{2,1,0:T(8,128)} copy(f32[64,24,2048]{2,0,1:T(8,128)} %bitcast.128) | data formatting | bytes 25165824 | tf_op jit(solution)/shard_map/reshape | solution.py:89
  257.1 8.0 %fusion.18 = f32[2,64,12,2048]{3,1,2,0:T(8,128)} fusion(bf16[64,2,12,384]{3,0,2,1:T(8,128)(2,1)} %get-tuple-element.16, bf16[2,384,2048]{2,1,0:T(8,128)(2,1)S(1)} %copy-done), kind=kOutput, calls=%fused_computation.28 | convolution fusion | flops 2415919104 | bytes 16908288 | tf_op jit(solution)/shard_map/slch,lhd->slcd/dot_general | solution.py:60
  265.1 16.3 %copy.36 = f32[64,24,2048]{2,1,0:T(8,128)} copy(f32[64,24,2048]{2,0,1:T(8,128)} %bitcast.127) | data formatting | bytes 25165824 | tf_op jit(solution)/shard_map/reshape | solution.py:61
  281.5 126.2 %reduce-scatter.5.cloned.1.call-done = f32[64,24,1024]{2,1,0:T(8,128)} async-done(((f32[64,24,2048]{2,1,0:T(8,128)}), f32[64,24,1024]{2,1,0:T(8,128)}) %reduce-scatter.5.cloned.1.call-update) | async-done | bytes 6291472 | tf_op jit(solution)/shard_map/reduce_scatter | solution.py:45
  407.7 4.9 convert_element_type.79
  412.6 9.9 %all-to-all-start.4 = ((bf16[64,24,1024]{2,1,0:T(8,128)(2,1)}), bf16[64,24,1024]{2,1,0:T(8,128)(2,1)S(1)}, u32[]{:S(2)}, u32[]{:S(2)}) async-start(bf16[64,24,1024]{2,1,0:T(8,128)(2,1)} %convert_element_type.79), calls=%async_computation.6 | async-start | bytes 6291456 | tf_op jit(solution)/shard_map/all_to_all | solution.py:48
  422.6 0.9 convert_element_type.80
  423.5 170.8 %reduce-scatter.3.cloned.1.call-done = f32[64,24,1024]{2,1,0:T(8,128)} async-done(((f32[64,24,2048]{2,1,0:T(8,128)}), f32[64,24,1024]{2,1,0:T(8,128)}) %reduce-scatter.3.cloned.1.call-update) | async-done | bytes 6291472 | tf_op jit(solution)/shard_map/reduce_scatter | solution.py:45
  594.2 4.9 convert_element_type.69
  599.1 7.9 %all-to-all-start.1 = ((bf16[64,24,1024]{2,1,0:T(8,128)(2,1)}), bf16[64,24,1024]{2,1,0:T(8,128)(2,1)}, u32[]{:S(2)}, u32[]{:S(2)}) async-start(bf16[64,24,1024]{2,1,0:T(8,128)(2,1)} %convert_element_type.69), calls=%async_computation.2 | async-start | bytes 6291456 | tf_op jit(solution)/shard_map/all_to_all | solution.py:48
  607.1 7.6 %bitcast_convert_fusion = bf16[2,384,2048]{2,1,0:T(8,128)(2,1)} fusion(bf16[64,2,12,384]{3,0,2,1:T(8,128)(2,1)} %get-tuple-element.16, bf16[64,2,12,2048]{3,0,2,1:T(8,128)(2,1)} %bitcast.138), kind=kOutput, calls=%fused_computation.6 | convolution fusion | flops 2417491968 | bytes 10616832 | tf_op jit(solution)/shard_map/slch,slcd->lhd/dot_general | solution.py:72
  614.7 8.1 %bitcast_convert_fusion.1 = bf16[2,2048,384]{2,1,0:T(8,128)(2,1)} fusion(bf16[64,2,12,2048]{3,0,2,1:T(8,128)(2,1)} %bitcast.133, bf16[64,2,12,384]{3,0,2,1:T(8,128)(2,1)S(1)} %copy-done.10), kind=kOutput, calls=%fused_computation.7 | convolution fusion | flops 2417491968 | bytes 10616832 | tf_op jit(solution)/shard_map/slcd,slch->ldh/dot_general | solution.py:83
  622.8 4.9 bitcast_convert_fusion.2
  627.7 5.4 gather_fusion.1
  633.1 3.7 bitcast_reduce_fusion
  636.8 11.5 %all-to-all-done.1 = bf16[64,24,1024]{2,1,0:T(8,128)(2,1)} async-done(((bf16[64,24,1024]{2,1,0:T(8,128)(2,1)}), bf16[64,24,1024]{2,1,0:T(8,128)(2,1)}, u32[]{:S(2)}, u32[]{:S(2)}) %all-to-all-start.1) | async-done | bytes 3145760 | tf_op jit(solution)/shard_map/all_to_all | solution.py:48
  648.3 8.5 %gather_fusion = bf16[1024,1024]{1,0:T(8,128)(2,1)} fusion(bf16[1536,1024]{1,0:T(8,128)(2,1)} %bitcast.18, s32[1024]{0:T(1024)S(1)} %broadcast_clamp_fusion), kind=kCustom, calls=%fused_computation | custom fusion | bytes 4198400 | tf_op jit(solution)/shard_map/gather | solution.py:49
  656.8 4.1 fusion.2
  660.8 9.5 %psum.7 = f32[128,8]{1,0:T(8,128)S(1)} all-reduce(f32[128,8]{1,0:T(8,128)S(1)} %get-tuple-element.12), channel_id=1, replica_groups=mesh['dp'=64,'col'=2] {'col'}, use_global_device_ids=true, to_apply=%region_10.11 | all-reduce | flops 1024 | bytes 8192 | tf_op jit(solution)/shard_map/psum | solution.py:91
  670.4 0.7 copy.42
  (49 shorter events, 0.7 us)
Async XLA Ops:
  7.2 214.7 %copy-start = (bf16[2,384,2048]{2,1,0:T(8,128)(2,1)S(1)}, bf16[2,384,2048]{2,1,0:T(8,128)(2,1)}, u32[]{:S(2)}) copy-start(bf16[2,384,2048]{2,1,0:T(8,128)(2,1)} %param.12) | copy-start | bytes 9437188
  9.3 19.8 %all-to-all-start.2 = ((bf16[2,128,1024]{1,2,0:T(8,128)(2,1)}), bf16[2,128,1024]{1,2,0:T(8,128)(2,1)}, u32[]{:S(2)}, u32[]{:S(2)}) async-start(bf16[2,128,1024]{1,2,0:T(8,128)(2,1)} %pad_maximum_fusion), calls=%async_computation.3 | async-start | bytes 1048576 | tf_op jit(solution)/shard_map/all_to_all | solution.py:9
  15.9 0.8 copy-start.8
  29.1 11.8 %copy-start.12 = (f32[128,8]{0,1:T(8,128)S(1)}, f32[128,8]{0,1:T(8,128)}, u32[]{:S(2)}) copy-start(f32[128,8]{0,1:T(8,128)} %param.9) | copy-start | bytes 12292
  29.1 94.5 %all-to-all-start = ((bf16[64,24,2048]{2,1,0:T(8,128)(2,1)}), bf16[64,24,2048]{2,1,0:T(8,128)(2,1)}, u32[]{:S(2)}, u32[]{:S(2)}) async-start(bf16[64,24,2048]{2,1,0:T(8,128)(2,1)} %bitcast.129), calls=%async_computation | async-start | bytes 12582912 | tf_op jit(solution)/shard_map/all_to_all | solution.py:40
  123.6 91.9 %all-to-all-start.3 = ((bf16[64,24,2048]{2,1,0:T(8,128)(2,1)}), bf16[64,24,2048]{2,1,0:T(8,128)(2,1)}, u32[]{:S(2)}, u32[]{:S(2)}) async-start(bf16[64,24,2048]{2,1,0:T(8,128)(2,1)} %bitcast.130), calls=%async_computation.4 | async-start | bytes 12582912 | tf_op jit(solution)/shard_map/all_to_all | solution.py:40
  132.4 275.3 %reduce-scatter.5.cloned.1.call-start = ((), (), s32[]{:S(2)}) async-start(), calls=%async_computation.8 | async-start | bytes 18874368 | tf_op jit(solution)/shard_map/reduce_scatter | solution.py:45
  132.6 6.4 copy-start.6
  139.0 4.8 copy-start.2
  139.1 4.8 copy-start.4
  215.5 6.4 copy-start.13
  215.5 6.4 copy-start.14
  221.8 6.1 copy-start.3
  221.9 6.0 copy-start.5
  227.9 4.9 copy-start.7
  257.0 337.2 %reduce-scatter.3.cloned.1.call-start = ((), (), s32[]{:S(2)}) async-start(), calls=%async_computation.7 | async-start | bytes 18874368 | tf_op jit(solution)/shard_map/reduce_scatter | solution.py:45
  412.6 9.9 %copy-start.11 = (bf16[128,1024]{1,0:T(8,128)(2,1)S(1)}, bf16[128,1024]{1,0:T(8,128)(2,1)}, u32[]{:S(2)}) copy-start(bf16[128,1024]{1,0:T(8,128)(2,1)} %param.13) | copy-start | bytes 786436
  412.6 186.5 %all-to-all-start.4 = ((bf16[64,24,1024]{2,1,0:T(8,128)(2,1)}), bf16[64,24,1024]{2,1,0:T(8,128)(2,1)S(1)}, u32[]{:S(2)}, u32[]{:S(2)}) async-start(bf16[64,24,1024]{2,1,0:T(8,128)(2,1)} %convert_element_type.79), calls=%async_computation.6 | async-start | bytes 6291456 | tf_op jit(solution)/shard_map/all_to_all | solution.py:48
  599.1 49.2 %all-to-all-start.1 = ((bf16[64,24,1024]{2,1,0:T(8,128)(2,1)}), bf16[64,24,1024]{2,1,0:T(8,128)(2,1)}, u32[]{:S(2)}, u32[]{:S(2)}) async-start(bf16[64,24,1024]{2,1,0:T(8,128)(2,1)} %convert_element_type.69), calls=%async_computation.2 | async-start | bytes 6291456 | tf_op jit(solution)/shard_map/all_to_all | solution.py:48
  607.1 7.6 %copy-start.10 = (bf16[64,2,12,384]{3,0,2,1:T(8,128)(2,1)S(1)}, bf16[64,2,12,384]{3,0,2,1:T(8,128)(2,1)}, u32[]{:S(2)}) copy-start(bf16[64,2,12,384]{3,0,2,1:T(8,128)(2,1)} %get-tuple-element.14) | copy-start | bytes 3538948
  607.1 15.7 %slice-start = ((s8[6291456]{0:T(1024)(128)(4,1)}), s8[4194304]{0:T(1024)(128)(4,1)S(1)}, s32[]{:S(2)}) async-start(s8[6291456]{0:T(1024)(128)(4,1)} %bitcast.134), calls=%async_computation.9 | async-start | bytes 8388608
  614.7 8.1 %slice-start.1 = ((s8[6291456]{0:T(1024)(128)(4,1)}), s8[2097152]{0:T(1024)(128)(4,1)S(1)}, s32[]{:S(2)}) async-start(s8[6291456]{0:T(1024)(128)(4,1)} %bitcast.134), calls=%async_computation.10 | async-start | bytes 4194304
  614.7 8.1 %copy-start.9 = (bf16[64,2,12,384]{3,0,2,1:T(8,128)(2,1)S(1)}, bf16[64,2,12,384]{3,0,2,1:T(8,128)(2,1)}, u32[]{:S(2)}) copy-start(bf16[64,2,12,384]{3,0,2,1:T(8,128)(2,1)} %get-tuple-element.15) | copy-start | bytes 3538948
  648.3 22.8 %copy-start.1 = (bf16[2,384,2048]{2,1,0:T(8,128)(2,1)S(1)}, bf16[2,384,2048]{2,1,0:T(8,128)(2,1)}, u32[]{:S(2)}) copy-start(bf16[2,384,2048]{2,1,0:T(8,128)(2,1)} %param.12) | copy-start | bytes 9437188
Sparse Core Ops, SparseCore 0:
  257.1 150.4 reduce-scatter.4
  410.1 184.0 reduce-scatter.2
